TPU v7x, 128 devices: a whole 4x4x4 slice. The times are simulated.
128 devices in a mesh: gz: 4 (over y_hi, core), tile: 32 (over y_lo, z, x).
Axes of the slice: x: 4, y: 4 (y_hi: 2, y_lo: 2; y = y_hi * 2 + y_lo), z: 4, core: 2. Of those that a mesh axis runs over, the one named last changes fastest.
Arguments:
- density: bfloat16 [32, 256, 512], P('gz', 'tile'), may hold values from -6 to 6
- w_first: bfloat16 [8, 1, 3, 3, 3], replicated, may hold values from -1.75 to 1.75
- b_first: float32 [8], replicated, may hold values from -1.25 to 1.25
- w_second: bfloat16 [8, 8, 3, 3, 3], replicated, may hold values from -0.5 to 0.5
- b_second: float32 [8], replicated, may hold values from -1.25 to 1.25
- w_third: bfloat16 [16, 8, 3, 3, 3], replicated, may hold values from -0.5 to 0.5
- b_third: float32 [16], replicated, may hold values from -1.25 to 1.25
- w_fourth: bfloat16 [16, 16, 3, 3, 3], replicated, may hold values from -0.4375 to 0.4375
- b_fourth: float32 [16], replicated, may hold values from -1.25 to 1.25
- w_fifth: bfloat16 [8, 24, 3, 3, 3], replicated, may hold values from -0.3125 to 0.3125
- b_fifth: float32 [8], replicated, may hold values from -1.25 to 1.25
- w_sixth: bfloat16 [8, 8, 3, 3, 3], replicated, may hold values from -0.5 to 0.5
- b_sixth: float32 [8], replicated, may hold values from -1.25 to 1.25
- w_head: bfloat16 [8], replicated, may hold values from -3 to 3
- b_head: float32 [1], replicated, may hold values from -1.75 to 1.75
Outputs:
- field: float32 [32, 256, 512], P('gz', 'tile')
All inputs are finite; a program needn't handle non-finite values.
Results may differ from a plain program's by a relative error of at most 0.012.
Values may be sent and summed in bfloat16 or wider, within the bound.
A program may use at most 128 MiB of HBM per device.

v0:
```python
import jax
import jax.numpy as jnp
from jax import lax
from jax.experimental import pallas as pl
from jax.experimental.pallas import tpu as pltpu
from jax.sharding import PartitionSpec as P

MESH = pl.DeviceIdType.MESH
F32 = jnp.float32
BF16 = jnp.bfloat16

ZL = 8
XL = 8
NY = 512
NC = NY // 2
WAYS = [(-1, -1), (-1, 1), (1, -1), (1, 1), (-1, 0), (1, 0), (0, -1), (0, 1)]


def lanes(shape):
    return lax.broadcasted_iota(jnp.int32, shape, len(shape) - 1)


def column(row, count):
    eye = lax.broadcasted_iota(jnp.int32, (count, count), 0) == lanes((count, count))
    return jnp.sum(jnp.where(eye, jnp.broadcast_to(row, (count, count)), 0.0), axis=1, keepdims=True)


def act(total):
    return jnp.maximum(total, 0.1 * total)


def spread_taps(weight, width, groups):
    taps, cout, cin = weight.shape
    rows = lax.broadcasted_iota(jnp.int32, (cin, width), 0)
    table = (lanes((cin, width)) % groups == rows).astype(F32).astype(BF16)
    flat = weight.astype(F32).reshape(taps * cout, cin).astype(BF16)
    return jnp.dot(flat, table, preferred_element_type=F32).reshape(taps, cout, width)


def store_band(dst, tiles, cin, outs, ins):
    cout, width = tiles.shape[1], tiles.shape[2]
    shape = (outs, cout, width)
    place = lanes(shape) // cin - lax.broadcasted_iota(jnp.int32, shape, 0)
    for dy in range(3):
        acc = jnp.zeros(shape, F32)
        for dz in range(3):
            for dx in range(3):
                tile = jnp.broadcast_to(tiles[dz * 9 + dx * 3 + dy][None], shape)
                acc = jnp.where(place == dz * ins + dx, tile, acc)
        rows = outs * cout
        dst[dy * rows : (dy + 1) * rows, :] = acc.reshape(rows, width).astype(BF16)


def fold(partial, rows, bias):
    width = partial.shape[1]
    low = pltpu.roll(partial[:rows], 1, 1)
    high = pltpu.roll(partial[2 * rows :], width - 1, 1)
    total = partial[rows : 2 * rows] + low + high
    cout = bias.shape[0]
    total = total.reshape(rows // cout, cout, width) + bias[None]
    return act(total).reshape(rows, width).astype(BF16)


def kernel(
    d_hbm, w1_h, b1_h, w2_h, b2_h, w3_h, b3_h, w4_h, b4_h, w5_h, b5_h, w6_h, b6_h, wh_h, bh_h,
    out_ref,
    w1, b1, w2, b2, w3, b3, w4, b4, w5, b5, w6, b6, wh, bh,
    dc, dl, dr, slo, shi, rolled, first, skip, pool_ex, pooled, one, upper, deco,
    m1, m2, m2s, m3, m4, m5, m6, mh, pick, spread, bias,
    in_sem, send1, recv1, send2, recv2,
):
    gz, tile = lax.axis_size("gz"), lax.axis_size("tile")
    g, t = lax.axis_index("gz"), lax.axis_index("tile")

    def neighbour(way):
        return (lax.rem(g + way[0] + gz, gz), lax.rem(t + way[1] + tile, tile))

    load_d = pltpu.make_async_copy(d_hbm, dc.at[4:12], in_sem.at[0])
    load_d.start()
    loads = []
    pairs = zip(
        (w1_h, b1_h, w2_h, b2_h, w3_h, b3_h, w4_h, b4_h, w5_h, b5_h, w6_h, b6_h, wh_h, bh_h),
        (w1, b1, w2, b2, w3, b3, w4, b4, w5, b5, w6, b6, wh, bh),
    )
    for i, (src, dst) in enumerate(pairs):
        loads.append(pltpu.make_async_copy(src, dst, in_sem.at[1 + i]))
        loads[-1].start()

    barrier = pltpu.get_barrier_semaphore()
    for way in WAYS:
        pl.semaphore_signal(barrier, inc=1, device_id=neighbour(way), device_id_type=MESH)

    load_d.wait()
    own = dc[4:12].astype(F32)
    slo[...] = own[:, :4].astype(BF16)
    shi[...] = own[:, 4:].astype(BF16)
    pl.semaphore_wait(barrier, len(WAYS))

    edge_src = {-1: (0, 4), 0: (0, 8), 1: (4, 4)}
    edge_dst = {-1: (12, 4), 0: (4, 8), 1: (0, 4)}
    copies = []
    for k, (sz, sx) in enumerate(WAYS):
        z0, n = edge_src[sz]
        d0, _ = edge_dst[sz]
        if sx == 0:
            src, dst = dc.at[4 + z0 : 4 + z0 + n], dc.at[d0 : d0 + n]
        else:
            src = (slo if sx < 0 else shi).at[z0 : z0 + n]
            dst = (dr if sx < 0 else dl).at[d0 : d0 + n]
        copies.append(
            pltpu.make_async_remote_copy(
                src_ref=src, dst_ref=dst, send_sem=send1.at[k], recv_sem=recv1.at[k],
                device_id=neighbour((sz, sx)), device_id_type=MESH,
            )
        )
        copies[-1].start()

    for load in loads:
        load.wait()
    for k, (ref, count) in enumerate(((b1, 8), (b2, 8), (b3, 16), (b4, 16), (b5, 8), (b6, 8))):
        bias[k, :count, :] = jnp.broadcast_to(column(ref[...], count), (count, NY))

    taps = w1[...].astype(F32)
    shape = (14, 8, 256)
    lane = lanes(shape)
    slot = lane % 16
    xx = jnp.where(slot < 8, slot + 4, jnp.where(slot < 12, slot - 8, slot))
    place = lane - slot + xx - lax.broadcasted_iota(jnp.int32, shape, 0)
    acc = jnp.zeros(shape, F32)
    for dz in range(3):
        for dx in range(3):
            for dy in range(3):
                col = column(taps[dz * 3 + dx, dy : dy + 1, :], 8)
                acc = jnp.where(place == dy * 48 + dz * 16 + dx, jnp.broadcast_to(col[None], shape), acc)
    m1[...] = acc.reshape(112, 256).astype(BF16)

    tiles = spread_taps(w2[...], 256, 8)
    store_band(m2, tiles, 8, 8, 10)
    store_band(m2s, tiles, 8, 2, 4)

    rows = lax.broadcasted_iota(jnp.int32, (8, 256), 0)
    table = (lanes((8, 256)) % 8 == rows).astype(F32).astype(BF16)
    w3v = w3[...]
    tiles = jnp.stack(
        [
            lax.dot_general(w3v[k], table, (((0,), (0,)), ((), ())), preferred_element_type=F32)
            for k in range(27)
        ]
    )
    store_band(m3, tiles, 8, 8, 10)
    store_band(m4, spread_taps(w4[...], 256, 16), 16, 3, 5)

    rows = lax.broadcasted_iota(jnp.int32, (24, 256), 0)
    lane = lanes((24, 256))
    table = jnp.where(lane < 144, lane % 8, (lane - 144) % 16 + 8) == rows
    flat = w5[...].astype(F32).reshape(27 * 8, 24).astype(BF16)
    tiles = jnp.dot(flat, table.astype(F32).astype(BF16), preferred_element_type=F32)
    tiles = tiles.reshape(27, 8, 256)
    shape = (4, 8, 256)
    lane = lanes(shape)
    out_x = lax.broadcasted_iota(jnp.int32, shape, 0)
    place = jnp.where(lane < 144, lane // 8 - out_x, -1)
    coarse = jnp.where(lane >= 144, (lane - 144) // 16, -1)
    for odd in range(2):
        for dy in range(3):
            acc = jnp.zeros(shape, F32)
            for dz in range(3):
                for dx in range(3):
                    tile_v = jnp.broadcast_to(tiles[dz * 9 + dx * 3 + dy][None], shape)
                    acc = jnp.where(place == dz * 6 + dx, tile_v, acc)
                    at = ((dz + odd) // 2) * 3 + (out_x + dx) // 2
                    acc = acc + jnp.where(coarse == at, tile_v, 0.0)
            m5[odd, dy * 32 : (dy + 1) * 32, :] = acc.reshape(32, 256).astype(BF16)

    store_band(m6, spread_taps(w6[...], 256, 8), 8, 8, 10)

    rows = lax.broadcasted_iota(jnp.int32, (8, 128), 0)
    lane = lanes((8, 128))
    table = (lane % 8 == rows).astype(F32).astype(BF16)
    head = jnp.dot(wh[...], table, preferred_element_type=F32)
    mh[...] = jnp.where(lane // 8 == rows, jnp.broadcast_to(head, (8, 128)), 0.0).astype(BF16)

    rows = lax.broadcasted_iota(jnp.int32, (NY, NC), 0)
    pick[...] = jnp.where(rows // 2 == lanes((NY, NC)), 0.125, 0.0).astype(BF16)
    rows = lax.broadcasted_iota(jnp.int32, (NC, NY), 0)
    spread[...] = jnp.where(lanes((NC, NY)) // 2 == rows, 1.0, 0.0).astype(BF16)

    for copy in copies:
        copy.wait()

    @pl.loop(0, 16)
    def _(z):
        full = jnp.concatenate(
            [dc[z].astype(F32), dl[z].astype(F32), dr[z].astype(F32)], axis=0
        )
        rolled[0, z] = pltpu.roll(full, 1, 1).astype(BF16)
        rolled[1, z] = full.astype(BF16)
        rolled[2, z] = pltpu.roll(full, NY - 1, 1).astype(BF16)

    def do_first(z):
        total = jnp.dot(
            m1[:, :144], rolled[:, pl.ds(z, 3)].reshape(144, NY), preferred_element_type=F32
        )
        total = total.reshape(14, 8, NY) + bias[0, :8, :][None]
        first[z] = act(total).reshape(112, NY).astype(BF16)

    def second_own(z):
        window = first[pl.ds(z, 3), 16:96].reshape(240, NY)
        out = fold(jnp.dot(m2[:, :240], window, preferred_element_type=F32), 64, bias[1, :8, :])
        skip[z, 16:80] = out
        return out

    def second_sides(z):
        for start, to in ((0, 0), (80, 80)):
            window = first[pl.ds(z, 3), start : start + 32].reshape(96, NY)
            skip[z, to : to + 16] = fold(
                jnp.dot(m2s[:, :96], window, preferred_element_type=F32), 16, bias[1, :8, :]
            )

    @pl.loop(2, 12)
    def _(z):
        do_first(z)

    @pl.loop(0, 4)
    def _(k):
        total = None
        for half in range(2):
            out = second_own(2 + 2 * k + half)
            part = jnp.dot(out, pick[...], preferred_element_type=F32)
            total = part if total is None else total + part
        pairs_x = total.reshape(4, 2, 8, NC)
        pool_ex[3 + k, 3:7] = (pairs_x[:, 0] + pairs_x[:, 1]).astype(BF16)

    edge_src = {-1: (3, 3), 0: (3, 4), 1: (4, 3)}
    edge_dst = {-1: 7, 0: 3, 1: 0}
    copies = []
    for k, (sz, sx) in enumerate(WAYS):
        z0, nz = edge_src[sz]
        x0, nx = edge_src[sx]
        zd, xd = edge_dst[sz], edge_dst[sx]
        copies.append(
            pltpu.make_async_remote_copy(
                src_ref=pool_ex.at[z0 : z0 + nz, x0 : x0 + nx],
                dst_ref=pool_ex.at[zd : zd + nz, xd : xd + nx],
                send_sem=send2.at[k], recv_sem=recv2.at[k],
                device_id=neighbour((sz, sx)), device_id_type=MESH,
            )
        )
        copies[-1].start()

    for z in (0, 1, 12, 13):
        do_first(z)

    @pl.loop(2, 10)
    def _(z):
        second_sides(z)

    for z in (0, 1, 10, 11):
        second_own(z)
        second_sides(z)

    for copy in copies:
        copy.wait()

    @pl.loop(0, 10)
    def _(z):
        pooled[z] = pool_ex[z].astype(F32).reshape(80, NC).astype(BF16)

    @pl.loop(0, 8)
    def _(z):
        window = pooled[pl.ds(z, 3)].reshape(240, NC)
        one[z] = fold(
            jnp.dot(m3[:, :240], window, preferred_element_type=F32), 128, bias[2, :, :NC]
        )

    @pl.loop(0, 6)
    def _(z):
        for b in range(2):
            window = one[pl.ds(z, 3), 48 * b : 48 * b + 80].reshape(240, NC)
            two = fold(
                jnp.dot(m4[:, :240], window, preferred_element_type=F32), 48, bias[3, :, :NC]
            )
            upper[z, 48 * b : 48 * b + 48] = jnp.dot(
                two, spread[...], preferred_element_type=F32
            ).astype(BF16)

    @pl.loop(0, 5)
    def _(k):
        for odd in range(2):
            z = 2 * k + odd
            for start, to, lo in ((0, 0, 0), (32, 32, 0), (48, 64, 16)):
                window = jnp.concatenate(
                    [
                        skip[pl.ds(z, 3), start : start + 48].reshape(144, NY),
                        upper[pl.ds(k, 2), start : start + 48].reshape(96, NY),
                    ],
                    axis=0,
                )
                band = m5[odd, :, :240]
                if lo:
                    band = jnp.concatenate([band[16:32], band[48:64], band[80:96]], axis=0)
                n = 32 - lo
                deco[z, to : to + n] = fold(
                    jnp.dot(band, window, preferred_element_type=F32), n, bias[4, :8, :]
                )

    @pl.loop(0, 8)
    def _(z):
        window = deco[pl.ds(z, 3)].reshape(240, NY)
        refined = fold(
            jnp.dot(m6[:, :240], window, preferred_element_type=F32), 64, bias[5, :8, :]
        )
        head = jnp.dot(mh[:, :64], refined, preferred_element_type=F32)
        out_ref[z] = head + jnp.broadcast_to(bh[...], (8, NY))


def body(d, w1, b1, w2, b2, w3, b3, w4, b4, w5, b5, w6, b6, wh, bh):
    def taps(weight, order):
        turned = weight.transpose(order)
        return turned.reshape(27, turned.shape[3], turned.shape[4])

    plain, swapped = (2, 3, 4, 0, 1), (2, 3, 4, 1, 0)
    args = (
        d,
        w1.transpose(1, 2, 3, 4, 0).reshape(9, 3, 8), b1.reshape(1, 8),
        taps(w2, plain), b2.reshape(1, 8),
        taps(w3, swapped), b3.reshape(1, 16),
        taps(w4, plain), b4.reshape(1, 16),
        taps(w5, plain), b5.reshape(1, 8),
        taps(w6, plain), b6.reshape(1, 8),
        wh.reshape(1, 8), bh.reshape(1, 1),
    )
    V = pltpu.VMEM
    small = [V(a.shape, a.dtype) for a in args[1:]]
    return pl.pallas_call(
        kernel,
        out_shape=jax.ShapeDtypeStruct((ZL, XL, NY), F32),
        in_specs=[pl.BlockSpec(memory_space=pl.ANY)] * len(args),
        out_specs=pl.BlockSpec(memory_space=pltpu.VMEM),
        scratch_shapes=small
        + [
            V((16, 8, NY), BF16), V((16, 4, NY), BF16), V((16, 4, NY), BF16),
            V((8, 4, NY), BF16), V((8, 4, NY), BF16),
            V((3, 16, 16, NY), BF16),
            V((14, 112, NY), BF16), V((12, 96, NY), BF16),
            V((10, 10, 8, NC), BF16), V((10, 80, NC), BF16),
            V((8, 128, NC), BF16), V((6, 96, NY), BF16), V((10, 80, NY), BF16),
            V((112, 256), BF16), V((192, 256), BF16), V((48, 256), BF16),
            V((384, 256), BF16), V((144, 256), BF16), V((2, 96, 256), BF16),
            V((192, 256), BF16), V((8, 128), BF16),
            V((NY, NC), BF16), V((NC, NY), BF16), V((6, 16, NY), F32),
            pltpu.SemaphoreType.DMA((15,)),
            pltpu.SemaphoreType.DMA((8,)), pltpu.SemaphoreType.DMA((8,)),
            pltpu.SemaphoreType.DMA((8,)), pltpu.SemaphoreType.DMA((8,)),
        ],
        compiler_params=pltpu.CompilerParams(
            collective_id=0, has_side_effects=True, vmem_limit_bytes=48 * 1024 * 1024
        ),
        name="unet_window",
    )(*args)


def solution(mesh):
    return jax.shard_map(
        body,
        mesh=mesh,
        in_specs=(P("gz", "tile", None),) + (P(),) * 14,
        out_specs=P("gz", "tile", None),
        check_vma=False,
    )
```

profile of v0, /device:TPU:1, one launch (start us, length us, event | category | flops | bytes accessed | tf_op | source)
XLA Modules:
  0.0 45.6 jit_solution(1211768907772115055)
XLA Ops:
  0.7 0.0 copy-start.6
  0.7 0.0 copy-start.10
  0.7 0.0 copy-start.11
  0.7 0.0 copy-start.12
  0.7 0.0 copy-start.13
  0.7 0.0 copy-start.7
  0.7 0.0 copy-start.8
  0.7 0.0 copy-start.9
  0.7 0.6 %copy-done.6 = bf16[8,1,3,3,3]{0,4,3,2,1:T(4,128)(2,1)S(1)} copy-done((bf16[8,1,3,3,3]{0,4,3,2,1:T(4,128)(2,1)S(1)}, bf16[8,1,3,3,3]{0,4,3,2,1:T(4,128)(2,1)}, u32[]{:S(2)}) %copy-start.6) | copy-done | bytes 456
  1.4 0.0 copy-done.10
  1.4 0.0 copy-done.11
  1.4 0.0 copy-done.12
  1.4 0.0 copy-done.13
  1.4 0.0 copy-done.7
  1.4 0.0 copy-done.8
  1.4 0.0 copy-done.9
  1.4 0.0 copy-start
  1.4 0.9 %copy-done = bf16[16,16,3,3,3]{1,0,4,3,2:T(8,128)(2,1)S(1)} copy-done((bf16[16,16,3,3,3]{1,0,4,3,2:T(8,128)(2,1)S(1)}, bf16[16,16,3,3,3]{1,0,4,3,2:T(8,128)(2,1)}, u32[]{:S(2)}) %copy-start) | copy-done | bytes 13848
  2.3 0.0 copy-start.1
  2.3 0.8 %copy-done.1 = bf16[8,8,512]{2,1,0:T(8,128)(2,1)S(1)} copy-done((bf16[8,8,512]{2,1,0:T(8,128)(2,1)S(1)}, bf16[8,8,512]{2,1,0:T(8,128)(2,1)}, u32[]{:S(2)}) %copy-start.1) | copy-done | bytes 65560
  3.2 0.0 copy-start.2
  3.2 0.8 %copy-done.2 = bf16[8,8,3,3,3]{1,0,4,3,2:T(8,128)(2,1)S(1)} copy-done((bf16[8,8,3,3,3]{1,0,4,3,2:T(8,128)(2,1)S(1)}, bf16[8,8,3,3,3]{1,0,4,3,2:T(8,128)(2,1)}, u32[]{:S(2)}) %copy-start.2) | copy-done | bytes 3480
  4.0 0.0 copy-start.3
  4.0 0.8 %copy-done.3 = bf16[16,8,3,3,3]{0,1,4,3,2:T(8,128)(2,1)S(1)} copy-done((bf16[16,8,3,3,3]{0,1,4,3,2:T(8,128)(2,1)S(1)}, bf16[16,8,3,3,3]{0,1,4,3,2:T(8,128)(2,1)}, u32[]{:S(2)}) %copy-start.3) | copy-done | bytes 6936
  4.8 0.0 copy-start.4
  4.8 0.8 %copy-done.4 = bf16[8,24,3,3,3]{1,0,4,3,2:T(8,128)(2,1)S(1)} copy-done((bf16[8,24,3,3,3]{1,0,4,3,2:T(8,128)(2,1)S(1)}, bf16[8,24,3,3,3]{1,0,4,3,2:T(8,128)(2,1)}, u32[]{:S(2)}) %copy-start.4) | copy-done | bytes 10392
  5.6 0.0 copy-start.5
  5.6 0.8 %copy-done.5 = bf16[8,8,3,3,3]{1,0,4,3,2:T(8,128)(2,1)S(1)} copy-done((bf16[8,8,3,3,3]{1,0,4,3,2:T(8,128)(2,1)S(1)}, bf16[8,8,3,3,3]{1,0,4,3,2:T(8,128)(2,1)}, u32[]{:S(2)}) %copy-start.5) | copy-done | bytes 3480
  6.4 38.6 %unet_window.1 = f32[8,8,512]{2,1,0:T(8,128)S(1)} custom-call(bf16[8,8,512]{2,1,0:T(8,128)(2,1)S(1)} %copy-done.1, bf16[9,3,8]{2,1,0:T(4,128)(2,1)S(1)} %bitcast.32, f32[1,8]{1,0:T(1,128)S(1)} %bitcast.33, bf16[27,8,8]{2,1,0:T(8,128)(2,1)S(1)} %bitcast.28, f32[1,8]{1,0:T(1,128)S(1)} %bitcast.34, bf16[27,8,16]{2,1,0:T(8,128)(2,1)S(1)} %bitcast.29, ...), custom_call_target="tpu_custom_call" | custom-call | tf_op jit(solution)/shard_map/unet_window/pallas_call | solution.py:335
  45.0 0.7 %copy.18 = f32[8,8,512]{2,1,0:T(8,128)} copy(f32[8,8,512]{2,1,0:T(8,128)S(1)} %unet_window.1) | data formatting | bytes 262144
Async XLA Ops:
  0.7 0.7 %copy-start.6 = (bf16[8,1,3,3,3]{0,4,3,2,1:T(4,128)(2,1)S(1)}, bf16[8,1,3,3,3]{0,4,3,2,1:T(4,128)(2,1)}, u32[]{:S(2)}) copy-start(bf16[8,1,3,3,3]{0,4,3,2,1:T(4,128)(2,1)} %param.16) | copy-start | bytes 1300
  0.7 0.7 %copy-start.10 = (f32[16]{0:T(128)S(1)}, f32[16]{0:T(128)}, u32[]{:S(2)}) copy-start(f32[16]{0:T(128)} %param.23) | copy-start | bytes 196
  0.7 0.7 %copy-start.11 = (f32[8]{0:T(128)S(1)}, f32[8]{0:T(128)}, u32[]{:S(2)}) copy-start(f32[8]{0:T(128)} %param.25) | copy-start | bytes 100
  0.7 0.7 %copy-start.12 = (f32[8]{0:T(128)S(1)}, f32[8]{0:T(128)}, u32[]{:S(2)}) copy-start(f32[8]{0:T(128)} %param.27) | copy-start | bytes 100
  0.7 0.7 %copy-start.13 = (bf16[8]{0:T(256)(128)(2,1)S(1)}, bf16[8]{0:T(256)(128)(2,1)}, u32[]{:S(2)}) copy-start(bf16[8]{0:T(256)(128)(2,1)} %param.28) | copy-start | bytes 52
  0.7 0.7 %copy-start.7 = (f32[8]{0:T(128)S(1)}, f32[8]{0:T(128)}, u32[]{:S(2)}) copy-start(f32[8]{0:T(128)} %param.17) | copy-start | bytes 100
  0.7 0.7 %copy-start.8 = (f32[8]{0:T(128)S(1)}, f32[8]{0:T(128)}, u32[]{:S(2)}) copy-start(f32[8]{0:T(128)} %param.19) | copy-start | bytes 100
  0.7 0.7 %copy-start.9 = (f32[16]{0:T(128)S(1)}, f32[16]{0:T(128)}, u32[]{:S(2)}) copy-start(f32[16]{0:T(128)} %param.21) | copy-start | bytes 196
  1.4 0.9 %copy-start = (bf16[16,16,3,3,3]{1,0,4,3,2:T(8,128)(2,1)S(1)}, bf16[16,16,3,3,3]{1,0,4,3,2:T(8,128)(2,1)}, u32[]{:S(2)}) copy-start(bf16[16,16,3,3,3]{1,0,4,3,2:T(8,128)(2,1)} %param.22) | copy-start | bytes 41476
  2.3 0.8 %copy-start.1 = (bf16[8,8,512]{2,1,0:T(8,128)(2,1)S(1)}, bf16[8,8,512]{2,1,0:T(8,128)(2,1)}, u32[]{:S(2)}) copy-start(bf16[8,8,512]{2,1,0:T(8,128)(2,1)} %d_hbm.1) | copy-start | bytes 196612
  3.2 0.8 %copy-start.2 = (bf16[8,8,3,3,3]{1,0,4,3,2:T(8,128)(2,1)S(1)}, bf16[8,8,3,3,3]{1,0,4,3,2:T(8,128)(2,1)}, u32[]{:S(2)}) copy-start(bf16[8,8,3,3,3]{1,0,4,3,2:T(8,128)(2,1)} %param.18) | copy-start | bytes 10372
  4.0 0.8 %copy-start.3 = (bf16[16,8,3,3,3]{0,1,4,3,2:T(8,128)(2,1)S(1)}, bf16[16,8,3,3,3]{0,1,4,3,2:T(8,128)(2,1)}, u32[]{:S(2)}) copy-start(bf16[16,8,3,3,3]{0,1,4,3,2:T(8,128)(2,1)} %param.20) | copy-start | bytes 20740
  4.8 0.8 %copy-start.4 = (bf16[8,24,3,3,3]{1,0,4,3,2:T(8,128)(2,1)S(1)}, bf16[8,24,3,3,3]{1,0,4,3,2:T(8,128)(2,1)}, u32[]{:S(2)}) copy-start(bf16[8,24,3,3,3]{1,0,4,3,2:T(8,128)(2,1)} %param.24) | copy-start | bytes 31108
  5.6 0.8 %copy-start.5 = (bf16[8,8,3,3,3]{1,0,4,3,2:T(8,128)(2,1)S(1)}, bf16[8,8,3,3,3]{1,0,4,3,2:T(8,128)(2,1)}, u32[]{:S(2)}) copy-start(bf16[8,8,3,3,3]{1,0,4,3,2:T(8,128)(2,1)} %param.26) | copy-start | bytes 10372
where the time goes:
time: 46.1 us; the launch traced here: 45.6 us
  Pallas kernels  38.6 us (84%)
  local copies, waits for them, and re-layouts  6.35 us (14%)
  between operations  0.73 us (2%)
    pallas_call x1, Pallas kernels, body(): pl.pallas_call(kernel, out_shape=jax.ShapeDtypeStruct((ZL, XL, NY), F32),...  38.6 us
    unnamed x29, local copies, waits for them, and re-layouts  6.35 us

commit v1 on v0

--- a/solution.py
+++ b/solution.py
@@ -14,6 +14,15 @@
 NY = 512
 NC = NY // 2
 WAYS = [(-1, -1), (-1, 1), (1, -1), (1, 1), (-1, 0), (1, 0), (0, -1), (0, 1)]
+
+U1 = 10
+U2 = 4
+U3 = 8
+UR = 5
+U4 = 8
+U5 = 6
+U6 = 5
+U7 = 8
 
 
 def lanes(shape):
@@ -51,12 +60,28 @@
         dst[dy * rows : (dy + 1) * rows, :] = acc.reshape(rows, width).astype(BF16)
 
 
+def loop(lo, hi, step, step_body):
+    assert (hi - lo) % step == 0
+
+    @pl.loop(0, (hi - lo) // step)
+    def _(k):
+        for u in range(step):
+            step_body(lo + k * step + u)
+
+
+def before(part):
+    return jnp.concatenate([pltpu.roll(part[:, -128:], 1, 1), part[:, :-128]], axis=1)
+
+
+def after(part):
+    return jnp.concatenate([part[:, 128:], pltpu.roll(part[:, :128], 127, 1)], axis=1)
+
+
 def fold(partial, rows, bias):
     width = partial.shape[1]
-    low = pltpu.roll(partial[:rows], 1, 1)
-    high = pltpu.roll(partial[2 * rows :], width - 1, 1)
-    total = partial[rows : 2 * rows] + low + high
+    total = partial[rows : 2 * rows] + before(partial[:rows]) + after(partial[2 * rows :])
     cout = bias.shape[0]
+    bias = jnp.concatenate([bias] * (width // 128), axis=1)
     total = total.reshape(rows // cout, cout, width) + bias[None]
     return act(total).reshape(rows, width).astype(BF16)
 
@@ -65,8 +90,8 @@
     d_hbm, w1_h, b1_h, w2_h, b2_h, w3_h, b3_h, w4_h, b4_h, w5_h, b5_h, w6_h, b6_h, wh_h, bh_h,
     out_ref,
     w1, b1, w2, b2, w3, b3, w4, b4, w5, b5, w6, b6, wh, bh,
-    dc, dl, dr, slo, shi, rolled, first, skip, pool_ex, pooled, one, upper, deco,
-    m1, m2, m2s, m3, m4, m5, m6, mh, pick, spread, bias,
+    d_in, dc, dl, dr, slo, shi, rolled, first, skip, pool_ex, pooled, one, two, deco, refined,
+    m1, m2, m2s, m3, m4, m5, m6, mh, mix, unmix, bias,
     in_sem, send1, recv1, send2, recv2,
 ):
     gz, tile = lax.axis_size("gz"), lax.axis_size("tile")
@@ -75,7 +100,11 @@
     def neighbour(way):
         return (lax.rem(g + way[0] + gz, gz), lax.rem(t + way[1] + tile, tile))
 
-    load_d = pltpu.make_async_copy(d_hbm, dc.at[4:12], in_sem.at[0])
+    barrier = pltpu.get_barrier_semaphore()
+    for way in WAYS:
+        pl.semaphore_signal(barrier, inc=1, device_id=neighbour(way), device_id_type=MESH)
+
+    load_d = pltpu.make_async_copy(d_hbm, d_in, in_sem.at[0])
     load_d.start()
     loads = []
     pairs = zip(
@@ -86,12 +115,12 @@
         loads.append(pltpu.make_async_copy(src, dst, in_sem.at[1 + i]))
         loads[-1].start()
 
-    barrier = pltpu.get_barrier_semaphore()
-    for way in WAYS:
-        pl.semaphore_signal(barrier, inc=1, device_id=neighbour(way), device_id_type=MESH)
-
+    rows = lax.broadcasted_iota(jnp.int32, (NY, NY), 0)
+    mix[...] = jnp.where(rows % 4 * 128 + rows // 4 == lanes((NY, NY)), 1.0, 0.0).astype(BF16)
     load_d.wait()
-    own = dc[4:12].astype(F32)
+    own = d_in[...].astype(F32).reshape(64, NY).astype(BF16)
+    own = jnp.dot(own, mix[...], preferred_element_type=F32).reshape(8, 8, NY)
+    dc[4:12] = own.astype(BF16)
     slo[...] = own[:, :4].astype(BF16)
     shi[...] = own[:, 4:].astype(BF16)
     pl.semaphore_wait(barrier, len(WAYS))
@@ -118,7 +147,7 @@
     for load in loads:
         load.wait()
     for k, (ref, count) in enumerate(((b1, 8), (b2, 8), (b3, 16), (b4, 16), (b5, 8), (b6, 8))):
-        bias[k, :count, :] = jnp.broadcast_to(column(ref[...], count), (count, NY))
+        bias[k, :count, :] = jnp.broadcast_to(column(ref[...], count), (count, 128))
 
     taps = w1[...].astype(F32)
     shape = (14, 8, 256)
@@ -180,10 +209,9 @@
     head = jnp.dot(wh[...], table, preferred_element_type=F32)
     mh[...] = jnp.where(lane // 8 == rows, jnp.broadcast_to(head, (8, 128)), 0.0).astype(BF16)
 
-    rows = lax.broadcasted_iota(jnp.int32, (NY, NC), 0)
-    pick[...] = jnp.where(rows // 2 == lanes((NY, NC)), 0.125, 0.0).astype(BF16)
-    rows = lax.broadcasted_iota(jnp.int32, (NC, NY), 0)
-    spread[...] = jnp.where(lanes((NC, NY)) // 2 == rows, 1.0, 0.0).astype(BF16)
+    lane = lanes((NY, NY))
+    rows = lax.broadcasted_iota(jnp.int32, (NY, NY), 0)
+    unmix[...] = jnp.where(lane % 4 * 128 + lane // 4 == rows, 1.0, 0.0).astype(BF16)
 
     for copy in copies:
         copy.wait()
@@ -193,15 +221,17 @@
         full = jnp.concatenate(
             [dc[z].astype(F32), dl[z].astype(F32), dr[z].astype(F32)], axis=0
         )
-        rolled[0, z] = pltpu.roll(full, 1, 1).astype(BF16)
+        rolled[0, z] = before(full).astype(BF16)
         rolled[1, z] = full.astype(BF16)
-        rolled[2, z] = pltpu.roll(full, NY - 1, 1).astype(BF16)
+        rolled[2, z] = after(full).astype(BF16)
+
+    wide_bias = jnp.concatenate([bias[0, :8, :]] * 4, axis=1)
 
     def do_first(z):
         total = jnp.dot(
             m1[:, :144], rolled[:, pl.ds(z, 3)].reshape(144, NY), preferred_element_type=F32
         )
-        total = total.reshape(14, 8, NY) + bias[0, :8, :][None]
+        total = total.reshape(14, 8, NY) + wide_bias[None]
         first[z] = act(total).reshape(112, NY).astype(BF16)
 
     def second_own(z):
@@ -217,19 +247,17 @@
                 jnp.dot(m2s[:, :96], window, preferred_element_type=F32), 16, bias[1, :8, :]
             )
 
-    @pl.loop(2, 12)
-    def _(z):
-        do_first(z)
-
-    @pl.loop(0, 4)
-    def _(k):
-        total = None
-        for half in range(2):
-            out = second_own(2 + 2 * k + half)
-            part = jnp.dot(out, pick[...], preferred_element_type=F32)
-            total = part if total is None else total + part
-        pairs_x = total.reshape(4, 2, 8, NC)
-        pool_ex[3 + k, 3:7] = (pairs_x[:, 0] + pairs_x[:, 1]).astype(BF16)
+    loop(2, 12, U1, do_first)
+    def own_pair(k):
+        total = second_own(2 + 2 * k).astype(F32) + second_own(3 + 2 * k).astype(F32)
+        total = total.reshape(4, 2, 8, NY)
+        total = total[:, 0] + total[:, 1]
+        low = total[:, :, :128] + total[:, :, 128:256]
+        high = total[:, :, 256:384] + total[:, :, 384:]
+        mean = jnp.concatenate([low, high], axis=2) * 0.125
+        pool_ex[3 + k, 3:7] = mean.astype(BF16)
+
+    loop(0, 4, U2, own_pair)
 
     edge_src = {-1: (3, 3), 0: (3, 4), 1: (4, 3)}
     edge_dst = {-1: 7, 0: 3, 1: 0}
@@ -250,11 +278,7 @@
 
     for z in (0, 1, 12, 13):
         do_first(z)
-
-    @pl.loop(2, 10)
-    def _(z):
-        second_sides(z)
-
+    loop(2, 10, U3, second_sides)
     for z in (0, 1, 10, 11):
         second_own(z)
         second_sides(z)
@@ -262,37 +286,33 @@
     for copy in copies:
         copy.wait()
 
-    @pl.loop(0, 10)
-    def _(z):
+    def repack(z):
         pooled[z] = pool_ex[z].astype(F32).reshape(80, NC).astype(BF16)
 
-    @pl.loop(0, 8)
-    def _(z):
+    def coarse_one(z):
         window = pooled[pl.ds(z, 3)].reshape(240, NC)
         one[z] = fold(
-            jnp.dot(m3[:, :240], window, preferred_element_type=F32), 128, bias[2, :, :NC]
-        )
-
-    @pl.loop(0, 6)
-    def _(z):
+            jnp.dot(m3[:, :240], window, preferred_element_type=F32), 128, bias[2]
+        )
+
+    def coarse_two(z):
         for b in range(2):
             window = one[pl.ds(z, 3), 48 * b : 48 * b + 80].reshape(240, NC)
-            two = fold(
-                jnp.dot(m4[:, :240], window, preferred_element_type=F32), 48, bias[3, :, :NC]
+            two[z, 48 * b : 48 * b + 48] = fold(
+                jnp.dot(m4[:, :240], window, preferred_element_type=F32), 48, bias[3]
             )
-            upper[z, 48 * b : 48 * b + 48] = jnp.dot(
-                two, spread[...], preferred_element_type=F32
-            ).astype(BF16)
-
-    @pl.loop(0, 5)
-    def _(k):
+
+    def repeat_y(part):
+        return jnp.concatenate([part[:, :128]] * 2 + [part[:, 128:]] * 2, axis=1)
+
+    def fifth(k):
         for odd in range(2):
             z = 2 * k + odd
             for start, to, lo in ((0, 0, 0), (32, 32, 0), (48, 64, 16)):
                 window = jnp.concatenate(
                     [
                         skip[pl.ds(z, 3), start : start + 48].reshape(144, NY),
-                        upper[pl.ds(k, 2), start : start + 48].reshape(96, NY),
+                        repeat_y(two[pl.ds(k, 2), start : start + 48].reshape(96, NC)),
                     ],
                     axis=0,
                 )
@@ -304,14 +324,27 @@
                     jnp.dot(band, window, preferred_element_type=F32), n, bias[4, :8, :]
                 )
 
-    @pl.loop(0, 8)
-    def _(z):
+    def sixth(z):
         window = deco[pl.ds(z, 3)].reshape(240, NY)
-        refined = fold(
+        refined[z] = fold(
             jnp.dot(m6[:, :240], window, preferred_element_type=F32), 64, bias[5, :8, :]
         )
-        head = jnp.dot(mh[:, :64], refined, preferred_element_type=F32)
-        out_ref[z] = head + jnp.broadcast_to(bh[...], (8, NY))
+
+    loop(0, 10, UR, repack)
+    loop(0, 8, U4, coarse_one)
+    loop(0, 6, U5, coarse_two)
+    loop(0, 5, U6, fifth)
+    loop(0, 8, U7, sixth)
+    head = jnp.concatenate(
+        [jnp.dot(mh[:, :64], refined[z], preferred_element_type=F32) for z in range(8)], axis=0
+    )
+    head = head + jnp.broadcast_to(bh[...], (64, NY))
+    parts = []
+    for _ in range(3):
+        parts.append(head.astype(BF16))
+        head = head - parts[-1].astype(F32)
+    plain = jnp.dot(jnp.concatenate(parts, axis=0), unmix[...], preferred_element_type=F32)
+    out_ref[...] = (plain[:64] + plain[64:128] + plain[128:]).reshape(8, 8, NY)
 
 
 def body(d, w1, b1, w2, b2, w3, b3, w4, b4, w5, b5, w6, b6, wh, bh):
@@ -339,22 +372,22 @@
         out_specs=pl.BlockSpec(memory_space=pltpu.VMEM),
         scratch_shapes=small
         + [
-            V((16, 8, NY), BF16), V((16, 4, NY), BF16), V((16, 4, NY), BF16),
+            V((8, 8, NY), BF16), V((16, 8, NY), BF16), V((16, 4, NY), BF16), V((16, 4, NY), BF16),
             V((8, 4, NY), BF16), V((8, 4, NY), BF16),
             V((3, 16, 16, NY), BF16),
             V((14, 112, NY), BF16), V((12, 96, NY), BF16),
             V((10, 10, 8, NC), BF16), V((10, 80, NC), BF16),
-            V((8, 128, NC), BF16), V((6, 96, NY), BF16), V((10, 80, NY), BF16),
+            V((8, 128, NC), BF16), V((6, 96, NC), BF16), V((10, 80, NY), BF16), V((8, 64, NY), BF16),
             V((112, 256), BF16), V((192, 256), BF16), V((48, 256), BF16),
             V((384, 256), BF16), V((144, 256), BF16), V((2, 96, 256), BF16),
             V((192, 256), BF16), V((8, 128), BF16),
-            V((NY, NC), BF16), V((NC, NY), BF16), V((6, 16, NY), F32),
+            V((NY, NY), BF16), V((NY, NY), BF16), V((6, 16, 128), F32),
             pltpu.SemaphoreType.DMA((15,)),
             pltpu.SemaphoreType.DMA((8,)), pltpu.SemaphoreType.DMA((8,)),
             pltpu.SemaphoreType.DMA((8,)), pltpu.SemaphoreType.DMA((8,)),
         ],
         compiler_params=pltpu.CompilerParams(
-            collective_id=0, has_side_effects=True, vmem_limit_bytes=48 * 1024 * 1024
+            collective_id=0, has_side_effects=True, vmem_limit_bytes=67043328
         ),
         name="unet_window",
     )(*args)

time: 46.1 us -> 29.9 us (0.65)
  Pallas kernels: 38.6 us -> 27.5 us
  local copies, waits for them, and re-layouts: 6.35 us -> 1.57 us
    pallas_call x1, Pallas kernels: 38.6 us -> 27.5 us  [body(): pl.pallas_call(kernel, out_shape=jax.ShapeDtypeStruct((ZL, XL, NY), F32),...]
    unnamed x29 -> x1, local copies, waits for them, and re-layouts: 6.35 us -> 1.57 us
where the time goes in v1:
time: 29.9 us; the launch traced here: 29.8 us
  Pallas kernels  27.5 us (92%)
  local copies, waits for them, and re-layouts  1.57 us (5%)
  between operations  0.66 us (2%)
    pallas_call x1, Pallas kernels, body(): pl.pallas_call(kernel, out_shape=jax.ShapeDtypeStruct((ZL, XL, NY), F32),...  27.5 us
    unnamed x1, local copies, waits for them, and re-layouts  1.57 us

profile of v1, /device:TPU:1, one launch (start us, length us, event | category | flops | bytes accessed | tf_op | source)
XLA Modules:
  0.0 29.8 jit_solution(14073857197722810482)
XLA Ops:
  0.7 27.5 %unet_window.1 = f32[8,8,512]{2,1,0:T(8,128)} custom-call(bf16[8,8,512]{2,1,0:T(8,128)(2,1)} %d_hbm.1, bf16[9,3,8]{2,1,0:T(4,128)(2,1)} %bitcast.32, f32[1,8]{1,0:T(1,128)} %bitcast.33, bf16[27,8,8]{2,1,0:T(8,128)(2,1)} %bitcast.28, f32[1,8]{1,0:T(1,128)} %bitcast.34, bf16[27,8,16]{2,1,0:T(8,128)(2,1)} %bitcast.29, f32[1,16]{1,0:T(1,128)} %bitcast.35, ...), custom_call_target="tpu_custom_call" | custom-call | tf_op jit(solution)/shard_map/unet_window/pallas_call | solution.py:368
  28.2 1.6 %copy.18 = f32[8,8,512]{2,1,0:T(8,128)} copy(f32[8,8,512]{2,1,0:T(8,128)} %unet_window.1) | data formatting | bytes 262144

commit v2 on v1

--- a/solution.py
+++ b/solution.py
@@ -15,9 +15,6 @@
 NC = NY // 2
 WAYS = [(-1, -1), (-1, 1), (1, -1), (1, 1), (-1, 0), (1, 0), (0, -1), (0, 1)]
 
-U1 = 10
-U2 = 4
-U3 = 8
 UR = 5
 U4 = 8
 U5 = 6
@@ -90,8 +87,8 @@
     d_hbm, w1_h, b1_h, w2_h, b2_h, w3_h, b3_h, w4_h, b4_h, w5_h, b5_h, w6_h, b6_h, wh_h, bh_h,
     out_ref,
     w1, b1, w2, b2, w3, b3, w4, b4, w5, b5, w6, b6, wh, bh,
-    d_in, dc, dl, dr, slo, shi, rolled, first, skip, pool_ex, pooled, one, two, deco, refined,
-    m1, m2, m2s, m3, m4, m5, m6, mh, mix, unmix, bias,
+    d_in, dc, dl, dr, slo, shi, own_y, rim_y, first, skip, pool_ex, pooled, one, two, deco, refined,
+    m1, m2, m3, m4, m5, m6, mh, mix, unmix, bias,
     in_sem, send1, recv1, send2, recv2,
 ):
     gz, tile = lax.axis_size("gz"), lax.axis_size("tile")
@@ -152,20 +149,20 @@
     taps = w1[...].astype(F32)
     shape = (14, 8, 256)
     lane = lanes(shape)
-    slot = lane % 16
-    xx = jnp.where(slot < 8, slot + 4, jnp.where(slot < 12, slot - 8, slot))
-    place = lane - slot + xx - lax.broadcasted_iota(jnp.int32, shape, 0)
+    slot = lane % 8
+    rim = jnp.where(slot < 4, slot, slot + 8)
+    xx = jnp.where(lane < 96, slot + 4, rim) - lax.broadcasted_iota(jnp.int32, shape, 0)
+    place = jnp.where((xx >= 0) & (xx < 3), lane % 96 // 8 * 8 + xx, -1)
     acc = jnp.zeros(shape, F32)
     for dz in range(3):
         for dx in range(3):
             for dy in range(3):
                 col = column(taps[dz * 3 + dx, dy : dy + 1, :], 8)
-                acc = jnp.where(place == dy * 48 + dz * 16 + dx, jnp.broadcast_to(col[None], shape), acc)
+                acc = jnp.where(place == dz * 32 + dy * 8 + dx, jnp.broadcast_to(col[None], shape), acc)
     m1[...] = acc.reshape(112, 256).astype(BF16)
 
     tiles = spread_taps(w2[...], 256, 8)
-    store_band(m2, tiles, 8, 8, 10)
-    store_band(m2s, tiles, 8, 2, 4)
+    store_band(m2, tiles, 8, 4, 6)
 
     rows = lax.broadcasted_iota(jnp.int32, (8, 256), 0)
     table = (lanes((8, 256)) % 8 == rows).astype(F32).astype(BF16)
@@ -213,77 +210,101 @@
     rows = lax.broadcasted_iota(jnp.int32, (NY, NY), 0)
     unmix[...] = jnp.where(lane % 4 * 128 + lane // 4 == rows, 1.0, 0.0).astype(BF16)
 
-    for copy in copies:
-        copy.wait()
-
-    @pl.loop(0, 16)
-    def _(z):
-        full = jnp.concatenate(
-            [dc[z].astype(F32), dl[z].astype(F32), dr[z].astype(F32)], axis=0
-        )
-        rolled[0, z] = before(full).astype(BF16)
-        rolled[1, z] = full.astype(BF16)
-        rolled[2, z] = after(full).astype(BF16)
-
     wide_bias = jnp.concatenate([bias[0, :8, :]] * 4, axis=1)
 
-    def do_first(z):
+    def turn(dst, z, rows8):
+        part = [before(rows8), rows8, after(rows8), jnp.zeros_like(rows8)]
+        dst[z] = jnp.concatenate(part, axis=0).astype(BF16)
+
+    def turn_own(z):
+        turn(own_y, z, dc[z].astype(F32))
+
+    def turn_rim(z):
+        turn(rim_y, z, jnp.concatenate([dl[z].astype(F32), dr[z].astype(F32)], axis=0))
+
+    def first_own(z):
         total = jnp.dot(
-            m1[:, :144], rolled[:, pl.ds(z, 3)].reshape(144, NY), preferred_element_type=F32
-        )
-        total = total.reshape(14, 8, NY) + wide_bias[None]
-        first[z] = act(total).reshape(112, NY).astype(BF16)
-
-    def second_own(z):
-        window = first[pl.ds(z, 3), 16:96].reshape(240, NY)
-        out = fold(jnp.dot(m2[:, :240], window, preferred_element_type=F32), 64, bias[1, :8, :])
-        skip[z, 16:80] = out
-        return out
-
-    def second_sides(z):
-        for start, to in ((0, 0), (80, 80)):
-            window = first[pl.ds(z, 3), start : start + 32].reshape(96, NY)
-            skip[z, to : to + 16] = fold(
-                jnp.dot(m2s[:, :96], window, preferred_element_type=F32), 16, bias[1, :8, :]
-            )
-
-    loop(2, 12, U1, do_first)
-    def own_pair(k):
-        total = second_own(2 + 2 * k).astype(F32) + second_own(3 + 2 * k).astype(F32)
-        total = total.reshape(4, 2, 8, NY)
+            m1[32:80, :96], own_y[pl.ds(z, 3)].reshape(96, NY), preferred_element_type=F32
+        )
+        first[z, 32:80] = act(total.reshape(6, 8, NY) + wide_bias[None]).reshape(48, NY).astype(BF16)
+
+    def first_rim(z):
+        band = jnp.concatenate([m1[0:32, :192], m1[80:112, :192]], axis=0)
+        window = jnp.concatenate(
+            [own_y[pl.ds(z, 3)].reshape(96, NY), rim_y[pl.ds(z, 3)].reshape(96, NY)], axis=0
+        )
+        total = jnp.dot(band, window, preferred_element_type=F32).reshape(8, 8, NY)
+        out = act(total + wide_bias[None]).reshape(64, NY).astype(BF16)
+        first[z, 0:32] = out[:32]
+        first[z, 80:112] = out[32:]
+
+    def second(z, b):
+        window = first[pl.ds(z, 3), 32 * b : 32 * b + 48].reshape(144, NY)
+        out = fold(jnp.dot(m2[:, :144], window, preferred_element_type=F32), 32, bias[1, :8, :])
+        skip[z, 32 * b : 32 * b + 32] = out
+        return out.astype(F32)
+
+    def pool(k, b):
+        total = (second(2 * k, b) + second(2 * k + 1, b)).reshape(2, 2, 8, NY)
         total = total[:, 0] + total[:, 1]
         low = total[:, :, :128] + total[:, :, 128:256]
         high = total[:, :, 256:384] + total[:, :, 384:]
         mean = jnp.concatenate([low, high], axis=2) * 0.125
-        pool_ex[3 + k, 3:7] = mean.astype(BF16)
-
-    loop(0, 4, U2, own_pair)
-
-    edge_src = {-1: (3, 3), 0: (3, 4), 1: (4, 3)}
-    edge_dst = {-1: 7, 0: 3, 1: 0}
-    copies = []
-    for k, (sz, sx) in enumerate(WAYS):
-        z0, nz = edge_src[sz]
-        x0, nx = edge_src[sx]
-        zd, xd = edge_dst[sz], edge_dst[sx]
-        copies.append(
+        pool_ex[2 + k, 2 + 2 * b : 4 + 2 * b] = mean.astype(BF16)
+
+    pool_src = {-1: (4, 6), 0: (2, 8), 1: (4, 6)}
+    pool_dst = {-1: (8, 10), 0: (2, 8), 1: (0, 2)}
+    copies2 = []
+    for k, (sz, sx) in enumerate(WAYS):
+        (z0, z1), (x0, x1) = pool_src[sz], pool_src[sx]
+        (y0, y1), (u0, u1) = pool_dst[sz], pool_dst[sx]
+        copies2.append(
             pltpu.make_async_remote_copy(
-                src_ref=pool_ex.at[z0 : z0 + nz, x0 : x0 + nx],
-                dst_ref=pool_ex.at[zd : zd + nz, xd : xd + nx],
+                src_ref=pool_ex.at[z0:z1, x0:x1],
+                dst_ref=pool_ex.at[y0:y1, u0:u1],
                 send_sem=send2.at[k], recv_sem=recv2.at[k],
                 device_id=neighbour((sz, sx)), device_id_type=MESH,
             )
         )
-        copies[-1].start()
-
-    for z in (0, 1, 12, 13):
-        do_first(z)
-    loop(2, 10, U3, second_sides)
-    for z in (0, 1, 10, 11):
-        second_own(z)
-        second_sides(z)
+
+    for k, (sz, sx) in enumerate(WAYS):
+        if sx == 0:
+            copies[k].wait_recv()
+    for z in range(16):
+        turn_own(z)
+    for z in range(14):
+        first_own(z)
+    for k in range(6):
+        pool(k, 1)
+    for k, (sz, sx) in enumerate(WAYS):
+        if sx != 0:
+            copies2[k].start()
+
+    for k, (sz, sx) in enumerate(WAYS):
+        if sx != 0:
+            copies[k].wait_recv()
+    for z in range(4, 12):
+        turn_rim(z)
+    for z in range(4, 10):
+        first_rim(z)
+    for k in (2, 3):
+        pool(k, 0)
+        pool(k, 2)
+    for k, (sz, sx) in enumerate(WAYS):
+        if sx == 0:
+            copies2[k].start()
+
+    for z in (0, 1, 2, 3, 12, 13, 14, 15):
+        turn_rim(z)
+    for z in (0, 1, 2, 3, 10, 11, 12, 13):
+        first_rim(z)
+    for k in (0, 1, 4, 5):
+        pool(k, 0)
+        pool(k, 2)
 
     for copy in copies:
+        copy.wait_send()
+    for copy in copies2:
         copy.wait()
 
     def repack(z):
@@ -374,11 +395,11 @@
         + [
             V((8, 8, NY), BF16), V((16, 8, NY), BF16), V((16, 4, NY), BF16), V((16, 4, NY), BF16),
             V((8, 4, NY), BF16), V((8, 4, NY), BF16),
-            V((3, 16, 16, NY), BF16),
+            V((16, 32, NY), BF16), V((16, 32, NY), BF16),
             V((14, 112, NY), BF16), V((12, 96, NY), BF16),
             V((10, 10, 8, NC), BF16), V((10, 80, NC), BF16),
             V((8, 128, NC), BF16), V((6, 96, NC), BF16), V((10, 80, NY), BF16), V((8, 64, NY), BF16),
-            V((112, 256), BF16), V((192, 256), BF16), V((48, 256), BF16),
+            V((112, 256), BF16), V((96, 256), BF16),
             V((384, 256), BF16), V((144, 256), BF16), V((2, 96, 256), BF16),
             V((192, 256), BF16), V((8, 128), BF16),
             V((NY, NY), BF16), V((NY, NY), BF16), V((6, 16, 128), F32),

time: 29.9 us -> 24.8 us (0.83)
  Pallas kernels: 27.5 us -> 22.4 us
    pallas_call x1, Pallas kernels: 27.5 us -> 22.4 us  [body(): pl.pallas_call(kernel, out_shape=jax.ShapeDtypeStruct((ZL, XL, NY), F32),...]
where the time goes in v2:
time: 24.8 us; the launch traced here: 24.6 us
  Pallas kernels  22.4 us (90%)
  local copies, waits for them, and re-layouts  1.57 us (6%)
  between operations  0.66 us (3%)
    pallas_call x1, Pallas kernels, body(): pl.pallas_call(kernel, out_shape=jax.ShapeDtypeStruct((ZL, XL, NY), F32),...  22.4 us
    unnamed x1, local copies, waits for them, and re-layouts  1.57 us

profile of v2, /device:TPU:1, one launch (start us, length us, event | category | flops | bytes accessed | tf_op | source)
XLA Modules:
  0.0 24.6 jit_solution(18180818696212938141)
XLA Ops:
  0.7 22.4 %unet_window.1 = f32[8,8,512]{2,1,0:T(8,128)} custom-call(bf16[8,8,512]{2,1,0:T(8,128)(2,1)} %d_hbm.1, bf16[9,3,8]{2,1,0:T(4,128)(2,1)} %bitcast.32, f32[1,8]{1,0:T(1,128)} %bitcast.33, bf16[27,8,8]{2,1,0:T(8,128)(2,1)} %bitcast.28, f32[1,8]{1,0:T(1,128)} %bitcast.34, bf16[27,8,16]{2,1,0:T(8,128)(2,1)} %bitcast.29, f32[1,16]{1,0:T(1,128)} %bitcast.35, ...), custom_call_target="tpu_custom_call" | custom-call | tf_op jit(solution)/shard_map/unet_window/pallas_call | solution.py:389
  23.1 1.6 %copy.18 = f32[8,8,512]{2,1,0:T(8,128)} copy(f32[8,8,512]{2,1,0:T(8,128)} %unet_window.1) | data formatting | bytes 262144

commit v3 on v2

--- a/solution.py
+++ b/solution.py
@@ -74,21 +74,25 @@
     return jnp.concatenate([part[:, 128:], pltpu.roll(part[:, :128], 127, 1)], axis=1)
 
 
-def fold(partial, rows, bias):
+def gather(partial, rows, bias):
     width = partial.shape[1]
     total = partial[rows : 2 * rows] + before(partial[:rows]) + after(partial[2 * rows :])
     cout = bias.shape[0]
     bias = jnp.concatenate([bias] * (width // 128), axis=1)
     total = total.reshape(rows // cout, cout, width) + bias[None]
-    return act(total).reshape(rows, width).astype(BF16)
+    return total.reshape(rows, width)
+
+
+def fold(partial, rows, bias):
+    return act(gather(partial, rows, bias)).astype(BF16)
 
 
 def kernel(
     d_hbm, w1_h, b1_h, w2_h, b2_h, w3_h, b3_h, w4_h, b4_h, w5_h, b5_h, w6_h, b6_h, wh_h, bh_h,
     out_ref,
     w1, b1, w2, b2, w3, b3, w4, b4, w5, b5, w6, b6, wh, bh,
-    d_in, dc, dl, dr, slo, shi, own_y, rim_y, first, skip, pool_ex, pooled, one, two, deco, refined,
-    m1, m2, m3, m4, m5, m6, mh, mix, unmix, bias,
+    d_in, dc, dl, dr, slo, shi, own_y, rim_y, first, skip, pool_ex, pooled, one, two, fine, deco, refined,
+    m1, m2, m3, m4, m5, m5c, m6, mh, mix, unmix, bias,
     in_sem, send1, recv1, send2, recv2,
 ):
     gz, tile = lax.axis_size("gz"), lax.axis_size("tile")
@@ -176,27 +180,28 @@
     store_band(m3, tiles, 8, 8, 10)
     store_band(m4, spread_taps(w4[...], 256, 16), 16, 3, 5)
 
+    flat = w5[...].astype(F32).reshape(27 * 8, 24).astype(BF16)
     rows = lax.broadcasted_iota(jnp.int32, (24, 256), 0)
     lane = lanes((24, 256))
-    table = jnp.where(lane < 144, lane % 8, (lane - 144) % 16 + 8) == rows
-    flat = w5[...].astype(F32).reshape(27 * 8, 24).astype(BF16)
-    tiles = jnp.dot(flat, table.astype(F32).astype(BF16), preferred_element_type=F32)
-    tiles = tiles.reshape(27, 8, 256)
-    shape = (4, 8, 256)
-    lane = lanes(shape)
+    table = (lane % 8 == rows).astype(F32).astype(BF16)
+    tiles = jnp.dot(flat, table, preferred_element_type=F32).reshape(27, 8, 256)
+    store_band(m5, tiles, 8, 4, 6)
+    table = (lane % 16 + 8 == rows).astype(F32).astype(BF16)
+    tiles = jnp.dot(flat, table, preferred_element_type=F32).reshape(27, 8, 256)
+    shape = (10, 8, 256)
+    coarse = lanes(shape) // 16
     out_x = lax.broadcasted_iota(jnp.int32, shape, 0)
-    place = jnp.where(lane < 144, lane // 8 - out_x, -1)
-    coarse = jnp.where(lane >= 144, (lane - 144) // 16, -1)
     for odd in range(2):
         for dy in range(3):
             acc = jnp.zeros(shape, F32)
-            for dz in range(3):
+            for zc in range(2):
                 for dx in range(3):
-                    tile_v = jnp.broadcast_to(tiles[dz * 9 + dx * 3 + dy][None], shape)
-                    acc = jnp.where(place == dz * 6 + dx, tile_v, acc)
-                    at = ((dz + odd) // 2) * 3 + (out_x + dx) // 2
-                    acc = acc + jnp.where(coarse == at, tile_v, 0.0)
-            m5[odd, dy * 32 : (dy + 1) * 32, :] = acc.reshape(32, 256).astype(BF16)
+                    near = [dz for dz in range(3) if (dz + odd) // 2 == zc]
+                    tile_v = sum(tiles[dz * 9 + dx * 3 + dy] for dz in near)
+                    hit = coarse == zc * 6 + (out_x + dx) // 2
+                    acc = acc + jnp.where(hit, jnp.broadcast_to(tile_v[None], shape), 0.0)
+            at = odd * 240 + dy * 80
+            m5c[at : at + 80, :] = acc.reshape(80, 256).astype(BF16)
 
     store_band(m6, spread_taps(w6[...], 256, 8), 8, 8, 10)
 
@@ -302,6 +307,20 @@
         pool(k, 0)
         pool(k, 2)
 
+    def fifth_skip(z):
+        for start, to, lo in ((0, 0, 0), (32, 32, 0), (48, 64, 16)):
+            window = skip[pl.ds(z, 3), start : start + 48].reshape(144, NY)
+            band = m5[:, :144]
+            if lo:
+                band = jnp.concatenate([band[16:32], band[48:64], band[80:96]], axis=0)
+            n = 32 - lo
+            fine[z, to : to + n] = gather(
+                jnp.dot(band, window, preferred_element_type=F32), n, bias[4, :8, :]
+            )
+
+    for z in range(10):
+        fifth_skip(z)
+
     for copy in copies:
         copy.wait_send()
     for copy in copies2:
@@ -323,27 +342,21 @@
                 jnp.dot(m4[:, :240], window, preferred_element_type=F32), 48, bias[3]
             )
 
-    def repeat_y(part):
-        return jnp.concatenate([part[:, :128]] * 2 + [part[:, 128:]] * 2, axis=1)
-
     def fifth(k):
+        window = two[pl.ds(k, 2)].reshape(192, NC)
+        parts = jnp.dot(m5c[:, :192], window, preferred_element_type=F32)
         for odd in range(2):
-            z = 2 * k + odd
-            for start, to, lo in ((0, 0, 0), (32, 32, 0), (48, 64, 16)):
-                window = jnp.concatenate(
-                    [
-                        skip[pl.ds(z, 3), start : start + 48].reshape(144, NY),
-                        repeat_y(two[pl.ds(k, 2), start : start + 48].reshape(96, NC)),
-                    ],
-                    axis=0,
-                )
-                band = m5[odd, :, :240]
-                if lo:
-                    band = jnp.concatenate([band[16:32], band[48:64], band[80:96]], axis=0)
-                n = 32 - lo
-                deco[z, to : to + n] = fold(
-                    jnp.dot(band, window, preferred_element_type=F32), n, bias[4, :8, :]
-                )
+            a = [parts[240 * odd + 80 * dy : 240 * odd + 80 * dy + 80, :128] for dy in range(3)]
+            b = [parts[240 * odd + 80 * dy : 240 * odd + 80 * dy + 80, 128:] for dy in range(3)]
+            both = a[0] + b[2]
+            blocks = [
+                a[1] + a[2] + pltpu.roll(b[0], 1, 1),
+                a[1] + both,
+                b[1] + both,
+                b[1] + b[0] + pltpu.roll(a[2], 127, 1),
+            ]
+            total = jnp.concatenate(blocks, axis=1) + fine[2 * k + odd]
+            deco[2 * k + odd] = act(total).astype(BF16)
 
     def sixth(z):
         window = deco[pl.ds(z, 3)].reshape(240, NY)
@@ -388,7 +401,7 @@
     small = [V(a.shape, a.dtype) for a in args[1:]]
     return pl.pallas_call(
         kernel,
-        out_shape=jax.ShapeDtypeStruct((ZL, XL, NY), F32),
+        out_shape=pltpu.VMEM((ZL, XL, NY), F32),
         in_specs=[pl.BlockSpec(memory_space=pl.ANY)] * len(args),
         out_specs=pl.BlockSpec(memory_space=pltpu.VMEM),
         scratch_shapes=small
@@ -398,9 +411,9 @@
             V((16, 32, NY), BF16), V((16, 32, NY), BF16),
             V((14, 112, NY), BF16), V((12, 96, NY), BF16),
             V((10, 10, 8, NC), BF16), V((10, 80, NC), BF16),
-            V((8, 128, NC), BF16), V((6, 96, NC), BF16), V((10, 80, NY), BF16), V((8, 64, NY), BF16),
+            V((8, 128, NC), BF16), V((6, 96, NC), BF16), V((10, 80, NY), F32), V((10, 80, NY), BF16), V((8, 64, NY), BF16),
             V((112, 256), BF16), V((96, 256), BF16),
-            V((384, 256), BF16), V((144, 256), BF16), V((2, 96, 256), BF16),
+            V((384, 256), BF16), V((144, 256), BF16), V((96, 256), BF16), V((480, 256), BF16),
             V((192, 256), BF16), V((8, 128), BF16),
             V((NY, NY), BF16), V((NY, NY), BF16), V((6, 16, 128), F32),
             pltpu.SemaphoreType.DMA((15,)),
@@ -408,7 +421,7 @@
             pltpu.SemaphoreType.DMA((8,)), pltpu.SemaphoreType.DMA((8,)),
         ],
         compiler_params=pltpu.CompilerParams(
-            collective_id=0, has_side_effects=True, vmem_limit_bytes=67043328
+            collective_id=0, has_side_effects=True, vmem_limit_bytes=67108864 - 196608
         ),
         name="unet_window",
     )(*args)

time: 24.8 us -> 22.5 us (0.907)
  Pallas kernels: 22.4 us -> 21.1 us
  local copies, waits for them, and re-layouts: 1.57 us -> 0.66 us
    pallas_call x1, Pallas kernels: 22.4 us -> 21.1 us  [body(): pl.pallas_call(kernel, out_shape=pltpu.VMEM((ZL, XL, NY), F32), in_specs=...]
    unnamed x1, local copies, waits for them, and re-layouts: 1.57 us -> 0.66 us
where the time goes in v3:
time: 22.5 us; the launch traced here: 22.4 us
  Pallas kernels  21.1 us (94%)
  local copies, waits for them, and re-layouts  0.66 us (3%)
  between operations  0.66 us (3%)
    pallas_call x1, Pallas kernels, body(): pl.pallas_call(kernel, out_shape=pltpu.VMEM((ZL, XL, NY), F32), in_specs=...  21.1 us
    unnamed x1, local copies, waits for them, and re-layouts  0.66 us

profile of v3, /device:TPU:1, one launch (start us, length us, event | category | flops | bytes accessed | tf_op | source)
XLA Modules:
  0.0 22.4 jit_solution(7599281017673712833)
XLA Ops:
  0.7 21.1 %unet_window.1 = f32[8,8,512]{2,1,0:T(8,128)S(1)} custom-call(bf16[8,8,512]{2,1,0:T(8,128)(2,1)} %d_hbm.1, bf16[9,3,8]{2,1,0:T(4,128)(2,1)} %bitcast.32, f32[1,8]{1,0:T(1,128)} %bitcast.33, bf16[27,8,8]{2,1,0:T(8,128)(2,1)} %bitcast.28, f32[1,8]{1,0:T(1,128)} %bitcast.34, bf16[27,8,16]{2,1,0:T(8,128)(2,1)} %bitcast.29, f32[1,16]{1,0:T(1,128)} %bitcast.35, ...), custom_call_target="tpu_custom_call" | custom-call | tf_op jit(solution)/shard_map/unet_window/pallas_call | solution.py:402
  21.7 0.7 %copy.17 = f32[8,8,512]{2,1,0:T(8,128)} copy(f32[8,8,512]{2,1,0:T(8,128)S(1)} %unet_window.1) | data formatting | bytes 262144

commit v4 on v3

--- a/solution.py
+++ b/solution.py
@@ -272,32 +272,57 @@
             )
         )
 
+    for z in range(4, 12):
+        turn_own(z)
+    for z in range(4, 10):
+        first_own(z)
+    for k in (2, 3):
+        pool(k, 1)
+
+    def middle():
+        for k, (sz, sx) in enumerate(WAYS):
+            if sx == 0:
+                copies[k].wait_recv()
+        for z in (0, 1, 2, 3, 12, 13, 14, 15):
+            turn_own(z)
+        for z in (0, 1, 2, 3, 10, 11, 12, 13):
+            first_own(z)
+        for k in (0, 1, 4, 5):
+            pool(k, 1)
+        for k, (sz, sx) in enumerate(WAYS):
+            if sx != 0:
+                copies2[k].start()
+
+    def layers():
+        for k, (sz, sx) in enumerate(WAYS):
+            if sz == 0:
+                copies[k].wait_recv()
+        for z in range(4, 12):
+            turn_rim(z)
+        for z in range(4, 10):
+            first_rim(z)
+        for k in (2, 3):
+            pool(k, 0)
+            pool(k, 2)
+        for k, (sz, sx) in enumerate(WAYS):
+            if sx == 0:
+                copies2[k].start()
+
+    row_start = lax.rem(t, 16) == 0
+
+    @pl.when(row_start)
+    def _():
+        layers()
+        middle()
+
+    @pl.when(jnp.logical_not(row_start))
+    def _():
+        middle()
+        layers()
+
     for k, (sz, sx) in enumerate(WAYS):
-        if sx == 0:
+        if sz != 0 and sx != 0:
             copies[k].wait_recv()
-    for z in range(16):
-        turn_own(z)
-    for z in range(14):
-        first_own(z)
-    for k in range(6):
-        pool(k, 1)
-    for k, (sz, sx) in enumerate(WAYS):
-        if sx != 0:
-            copies2[k].start()
-
-    for k, (sz, sx) in enumerate(WAYS):
-        if sx != 0:
-            copies[k].wait_recv()
-    for z in range(4, 12):
-        turn_rim(z)
-    for z in range(4, 10):
-        first_rim(z)
-    for k in (2, 3):
-        pool(k, 0)
-        pool(k, 2)
-    for k, (sz, sx) in enumerate(WAYS):
-        if sx == 0:
-            copies2[k].start()
 
     for z in (0, 1, 2, 3, 12, 13, 14, 15):
         turn_rim(z)

time: 22.5 us -> 21.9 us (0.973)
  Pallas kernels: 21.1 us -> 20.4 us
    pallas_call x1, Pallas kernels: 21.1 us -> 20.4 us  [body(): pl.pallas_call(kernel, out_shape=pltpu.VMEM((ZL, XL, NY), F32), in_specs=...]
where the time goes in v4:
time: 21.9 us; the launch traced here: 21.7 us
  Pallas kernels  20.4 us (93%)
  local copies, waits for them, and re-layouts  0.66 us (3%)
  between operations  0.66 us (3%)
    pallas_call x1, Pallas kernels, body(): pl.pallas_call(kernel, out_shape=pltpu.VMEM((ZL, XL, NY), F32), in_specs=...  20.4 us
    unnamed x1, local copies, waits for them, and re-layouts  0.66 us

profile of v4, /device:TPU:1, one launch (start us, length us, event | category | flops | bytes accessed | tf_op | source)
XLA Modules:
  0.0 21.7 jit_solution(5516545633604324870)
XLA Ops:
  0.7 20.4 %unet_window.1 = f32[8,8,512]{2,1,0:T(8,128)S(1)} custom-call(bf16[8,8,512]{2,1,0:T(8,128)(2,1)} %d_hbm.1, bf16[9,3,8]{2,1,0:T(4,128)(2,1)} %bitcast.32, f32[1,8]{1,0:T(1,128)} %bitcast.33, bf16[27,8,8]{2,1,0:T(8,128)(2,1)} %bitcast.28, f32[1,8]{1,0:T(1,128)} %bitcast.34, bf16[27,8,16]{2,1,0:T(8,128)(2,1)} %bitcast.29, f32[1,16]{1,0:T(1,128)} %bitcast.35, ...), custom_call_target="tpu_custom_call" | custom-call | tf_op jit(solution)/shard_map/unet_window/pallas_call | solution.py:427
  21.1 0.7 %copy.17 = f32[8,8,512]{2,1,0:T(8,128)} copy(f32[8,8,512]{2,1,0:T(8,128)S(1)} %unet_window.1) | data formatting | bytes 262144

commit v5 on v4

--- a/solution.py
+++ b/solution.py
@@ -257,12 +257,16 @@
         mean = jnp.concatenate([low, high], axis=2) * 0.125
         pool_ex[2 + k, 2 + 2 * b : 4 + 2 * b] = mean.astype(BF16)
 
-    pool_src = {-1: (4, 6), 0: (2, 8), 1: (4, 6)}
-    pool_dst = {-1: (8, 10), 0: (2, 8), 1: (0, 2)}
+    pool_src = {-1: (4, 6), 1: (4, 6)}
+    pool_dst = {-1: (8, 10), 1: (0, 2)}
+    pieces = [(way, pool_src[way[0]], pool_src[way[1]]) for way in WAYS[:4]]
+    pieces += [((sz, 0), (4, 6), (4, 6)) for sz in (-1, 1)]
+    pieces += [((0, sx), (2, 8), (4, 6)) for sx in (-1, 1)]
+    pieces += [((sz, 0), (4, 6), (x, x + 2)) for sz in (-1, 1) for x in (2, 6)]
     copies2 = []
-    for k, (sz, sx) in enumerate(WAYS):
-        (z0, z1), (x0, x1) = pool_src[sz], pool_src[sx]
-        (y0, y1), (u0, u1) = pool_dst[sz], pool_dst[sx]
+    for k, ((sz, sx), (z0, z1), (x0, x1)) in enumerate(pieces):
+        y0, y1 = pool_dst.get(sz, (z0, z1))
+        u0, u1 = pool_dst.get(sx, (x0, x1))
         copies2.append(
             pltpu.make_async_remote_copy(
                 src_ref=pool_ex.at[z0:z1, x0:x1],
@@ -278,6 +282,8 @@
         first_own(z)
     for k in (2, 3):
         pool(k, 1)
+    for copy in copies2[:6]:
+        copy.start()
 
     def middle():
         for k, (sz, sx) in enumerate(WAYS):
@@ -289,9 +295,8 @@
             first_own(z)
         for k in (0, 1, 4, 5):
             pool(k, 1)
-        for k, (sz, sx) in enumerate(WAYS):
-            if sx != 0:
-                copies2[k].start()
+        for copy in copies2[6:8]:
+            copy.start()
 
     def layers():
         for k, (sz, sx) in enumerate(WAYS):
@@ -304,9 +309,8 @@
         for k in (2, 3):
             pool(k, 0)
             pool(k, 2)
-        for k, (sz, sx) in enumerate(WAYS):
-            if sx == 0:
-                copies2[k].start()
+        for copy in copies2[8:]:
+            copy.start()
 
     row_start = lax.rem(t, 16) == 0
 
@@ -443,7 +447,7 @@
             V((NY, NY), BF16), V((NY, NY), BF16), V((6, 16, 128), F32),
             pltpu.SemaphoreType.DMA((15,)),
             pltpu.SemaphoreType.DMA((8,)), pltpu.SemaphoreType.DMA((8,)),
-            pltpu.SemaphoreType.DMA((8,)), pltpu.SemaphoreType.DMA((8,)),
+            pltpu.SemaphoreType.DMA((12,)), pltpu.SemaphoreType.DMA((12,)),
         ],
         compiler_params=pltpu.CompilerParams(
             collective_id=0, has_side_effects=True, vmem_limit_bytes=67108864 - 196608

time: 21.9 us -> 21.8 us (level)
  no operation moved by 1% of the time
where the time goes in v5:
time: 21.8 us; the launch traced here: 21.7 us
  Pallas kernels  20.3 us (93%)
  local copies, waits for them, and re-layouts  0.66 us (3%)
  between operations  0.66 us (3%)
    pallas_call x1, Pallas kernels, body(): pl.pallas_call(kernel, out_shape=pltpu.VMEM((ZL, XL, NY), F32), in_specs=...  20.3 us
    unnamed x1, local copies, waits for them, and re-layouts  0.66 us

profile of v5, /device:TPU:1, one launch (start us, length us, event | category | flops | bytes accessed | tf_op | source)
XLA Modules:
  0.0 21.7 jit_solution(884265171163771747)
XLA Ops:
  0.7 20.3 %unet_window.1 = f32[8,8,512]{2,1,0:T(8,128)S(1)} custom-call(bf16[8,8,512]{2,1,0:T(8,128)(2,1)} %d_hbm.1, bf16[9,3,8]{2,1,0:T(4,128)(2,1)} %bitcast.32, f32[1,8]{1,0:T(1,128)} %bitcast.33, bf16[27,8,8]{2,1,0:T(8,128)(2,1)} %bitcast.28, f32[1,8]{1,0:T(1,128)} %bitcast.34, bf16[27,8,16]{2,1,0:T(8,128)(2,1)} %bitcast.29, f32[1,16]{1,0:T(1,128)} %bitcast.35, ...), custom_call_target="tpu_custom_call" | custom-call | tf_op jit(solution)/shard_map/unet_window/pallas_call | solution.py:431
  21.0 0.7 %copy.17 = f32[8,8,512]{2,1,0:T(8,128)} copy(f32[8,8,512]{2,1,0:T(8,128)S(1)} %unet_window.1) | data formatting | bytes 262144

commit v6 on v5

--- a/solution.py
+++ b/solution.py
@@ -403,11 +403,11 @@
     )
     head = head + jnp.broadcast_to(bh[...], (64, NY))
     parts = []
-    for _ in range(3):
+    for _ in range(2):
         parts.append(head.astype(BF16))
         head = head - parts[-1].astype(F32)
     plain = jnp.dot(jnp.concatenate(parts, axis=0), unmix[...], preferred_element_type=F32)
-    out_ref[...] = (plain[:64] + plain[64:128] + plain[128:]).reshape(8, 8, NY)
+    out_ref[...] = (plain[:64] + plain[64:]).reshape(8, 8, NY)
 
 
 def body(d, w1, b1, w2, b2, w3, b3, w4, b4, w5, b5, w6, b6, wh, bh):

time: 21.8 us -> 21.8 us (level)
  no operation moved by 1% of the time
where the time goes in v6:
time: 21.8 us; the launch traced here: 21.6 us
  Pallas kernels  20.3 us (93%)
  local copies, waits for them, and re-layouts  0.66 us (3%)
  between operations  0.66 us (3%)
    pallas_call x1, Pallas kernels, body(): pl.pallas_call(kernel, out_shape=pltpu.VMEM((ZL, XL, NY), F32), in_specs=...  20.3 us
    unnamed x1, local copies, waits for them, and re-layouts  0.66 us

profile of v6, /device:TPU:1, one launch (start us, length us, event | category | flops | bytes accessed | tf_op | source)
XLA Modules:
  0.0 21.6 jit_solution(16681004528434422794)
XLA Ops:
  0.7 20.3 %unet_window.1 = f32[8,8,512]{2,1,0:T(8,128)S(1)} custom-call(bf16[8,8,512]{2,1,0:T(8,128)(2,1)} %d_hbm.1, bf16[9,3,8]{2,1,0:T(4,128)(2,1)} %bitcast.32, f32[1,8]{1,0:T(1,128)} %bitcast.33, bf16[27,8,8]{2,1,0:T(8,128)(2,1)} %bitcast.28, f32[1,8]{1,0:T(1,128)} %bitcast.34, bf16[27,8,16]{2,1,0:T(8,128)(2,1)} %bitcast.29, f32[1,16]{1,0:T(1,128)} %bitcast.35, ...), custom_call_target="tpu_custom_call" | custom-call | tf_op jit(solution)/shard_map/unet_window/pallas_call | solution.py:431
  21.0 0.7 %copy.17 = f32[8,8,512]{2,1,0:T(8,128)} copy(f32[8,8,512]{2,1,0:T(8,128)S(1)} %unet_window.1) | data formatting | bytes 262144
